TPU v7x, 512 devices: a whole 4x8x8 slice. The times are simulated.
512 devices in a mesh: mem: 16 (over z_hi, y), reg: 32 (over x, z_lo, core).
Axes of the slice: x: 4, y: 8, z: 8 (z_hi: 2, z_lo: 4; z = z_hi * 4 + z_lo), core: 2. Of those that a mesh axis runs over, the one named last changes fastest.
Arguments:
- ensemble: float32 [256, 131072], P('mem', 'reg'), may hold values from -6 to 6
- obs_pert: float32 [256, 32768], P('mem', 'reg'), may hold values from -45 to 45
- innovation: float32 [32768], P('reg'), may hold values from -6 to 6
- block_list: int32 [512, 8], P(('reg', 'mem')), may hold values from 0 to 255, as said below
- loc_weights: float32 [512, 8, 128], P(('reg', 'mem')), may hold values from 0.05 to 1
Outputs:
- analysis: float32 [256, 131072], P('mem', 'reg')
Inputs may be any that keep to these rules, and one draw needn't show every extreme that they name: `block_list`: each patch lists 8 different blocks. The regions split the patches and the blocks each into equal runs in order; a patch lists only blocks of its own region and of the regions just before and after it, and always the first and the last block of its own region.
All inputs are finite; a program needn't handle non-finite values.
Results may differ from a plain program's by a relative error of at most 0.0003.
Values sent between devices are 32-bit elements; how exact they have to be, the bound alone decides.
No kernel may reach another device: no remote copies, remote signals or barrier semaphores. Data moves between devices by JAX's collectives and lax.ppermute only.
A program may use at most 64 MiB of HBM per device.

v0:
```python
import jax
import jax.numpy as jnp
from jax import lax
from jax.experimental import pallas as pl
from jax.experimental.pallas import tpu as pltpu
from jax.sharding import Mesh
from jax.sharding import PartitionSpec as P


NEWTON = 8
LANES = 128
TILE = 8
HALVES = 2
FIXED = 2
F32 = jnp.float32
BF16 = jnp.bfloat16
I32 = jnp.int32
MEM = ("half", "ring")


def whole(count):
    return [pl.BlockSpec(memory_space=pltpu.VMEM)] * count


def near(*arrays):
    return [pltpu.with_memory_space_constraint(value, pltpu.VMEM) for value in arrays]


def pack(ensemble, obs_pert, block_list):
    rows, columns = ensemble.shape
    obs = obs_pert.shape[1]
    slots = block_list.shape[1]
    ring = lax.axis_size("ring")
    width = columns // (HALVES * ring)
    pieces = width // LANES
    depth = (HALVES * pieces + FIXED) * rows + TILE

    def kernel(ens_ref, obs_ref, list_ref, out_ref):
        half = lax.axis_index("half")
        for target in range(ring):
            at = target * depth
            for other in range(HALVES):
                patch = (half ^ other) * ring + target
                for piece in range(pieces):
                    start = pl.multiple_of(patch * width + piece * LANES, LANES)
                    out_ref[at : at + rows, :] = ens_ref[:, pl.ds(start, LANES)]
                    at += rows
            for start in (0, obs - LANES):
                out_ref[at : at + rows, :] = obs_ref[:, start : start + LANES]
                at += rows
            out_ref[at : at + TILE, :] = jnp.zeros((TILE, LANES), F32)
            out_ref[at : at + 1, 0:slots] = list_ref[...].astype(F32)

    return pl.pallas_call(
        kernel,
        out_shape=pltpu.VMEM((ring * depth, LANES), F32),
        in_specs=whole(3),
        out_specs=pl.BlockSpec(memory_space=pltpu.VMEM),
        name="pack",
    )(ensemble, obs_pert, block_list)


def select(listed, slots, weights, own, near_side, far_side):
    members = own.shape[0] - 1
    blocks = own.shape[1] // LANES
    others = slots - FIXED
    ring = lax.axis_size("ring")
    depth = listed.shape[0] // ring
    fixed = (blocks, 2 * blocks - 1)

    def kernel(
        listed_ref, weights_ref, own_ref, near_ref, far_ref, out_ref, scales_ref,
        table, innov_table, lists, staged, wanted, rest, list_sem, sems,
    ):
        region = lax.axis_index("reg")
        offset = (region - 1) * blocks
        odd = lax.rem(region, 2)
        for source in range(ring):
            at = (source + 1) * depth - TILE
            lists[source : source + 1, :] = listed_ref[at : at + 1, :].astype(I32) - offset
        copy = pltpu.make_async_copy(lists, wanted, list_sem)
        copy.start()
        for side, ref in ((1, own_ref), (2 - 2 * odd, near_ref), (2 * odd, far_ref)):
            for block in range(blocks):
                at = side * blocks + block
                table[at] = ref[0:members, block * LANES : (block + 1) * LANES]
                innov_table[at] = ref[members : members + 1, block * LANES : (block + 1) * LANES]
        copy.wait()

        def compact(patch, order):
            count = jnp.int32(0)
            places = [jnp.int32(0)] * FIXED
            for slot in range(slots):
                block = wanted[patch, slot]
                rest[order, count] = block
                if order:
                    rest[2, count] = jnp.int32(slot)
                    places = [jnp.where(block == f, slot, at) for f, at in zip(fixed, places)]
                found = [block == f for f in fixed]
                count = count + jnp.where(found[0] | found[1], 0, 1)
            return places

        copies = []
        for patch in range(ring):
            compact(patch, 0)
            for slot in range(others):
                staged[patch * members : (patch + 1) * members, slot * LANES : (slot + 1) * LANES] = table[rest[0, slot]]
            span = pl.ds(patch * members, members)
            copies.append(pltpu.make_async_copy(staged.at[span], out_ref.at[span], sems.at[patch]))
            copies[-1].start()
        places = compact(lax.axis_index("ring"), 1)
        for slot in range(others):
            scales_ref[slot : slot + 1, :] = innov_table[rest[1, slot]]
            scales_ref[slots + slot : slots + slot + 1, :] = weights_ref[pl.ds(rest[2, slot], 1), :]
        for which in range(FIXED):
            slot = others + which
            scales_ref[slot : slot + 1, :] = innov_table[fixed[which]]
            scales_ref[slots + slot : slots + slot + 1, :] = weights_ref[pl.ds(places[which], 1), :]
        for copy in copies:
            copy.wait()

    return pl.pallas_call(
        kernel,
        out_shape=(
            jax.ShapeDtypeStruct((ring * members, others * LANES), F32),
            pltpu.VMEM((2 * slots, LANES), F32),
        ),
        in_specs=whole(5),
        out_specs=(pl.BlockSpec(memory_space=pl.ANY), pl.BlockSpec(memory_space=pltpu.VMEM)),
        scratch_shapes=[
            pltpu.VMEM((3 * blocks, members, LANES), F32),
            pltpu.VMEM((3 * blocks, 1, LANES), F32),
            pltpu.VMEM((ring, LANES), I32),
            pltpu.VMEM((ring * members, others * LANES), F32),
            pltpu.SMEM((ring, LANES), I32),
            pltpu.SMEM((3, slots), I32),
            pltpu.SemaphoreType.DMA,
            pltpu.SemaphoreType.DMA((ring,)),
        ],
        name="select",
    )(*near(listed, weights, own, near_side, far_side))


def parts(value):
    high = value.astype(BF16)
    return high, (value - high.astype(F32)).astype(BF16)


def product(first, second):
    high1, low1 = first
    high2, low2 = second
    dot = lambda a, b: jnp.dot(a, b, preferred_element_type=F32)
    rows = high1.shape[0] // 2
    done = []
    for at in range(0, high1.shape[0], rows):
        low, high = low1[at : at + rows], high1[at : at + rows]
        both = dot(jnp.concatenate([low, high], axis=0), high2)
        done.append(both[rows:] + (both[0:rows] + dot(high, low2)))
    return jnp.concatenate(done, axis=0)


def scale(block, scales, slot, slots):
    roots = jnp.sqrt(scales[slots + slot : slots + slot + 1, :])
    scaled = block * roots
    return parts(scaled), scaled * (roots * scales[slot : slot + 1, :])


def contract(first, second):
    return lax.dot_general(first, second, (((1,), (1,)), ((), ())), preferred_element_type=F32)


def gram(pieces):
    high, low = (jnp.concatenate(piece, axis=1) for piece in zip(*pieces))
    cross = contract(high, low)
    return contract(high, high) + (cross + cross.T)


def prepare(scales, packed, crossed, rows):
    slots = scales.shape[0] // 2
    ring = lax.axis_size("ring")
    members = HALVES * ring * rows
    depth = packed.shape[0] // ring
    strips = crossed.shape[0] // (ring * rows)
    pieces = strips - FIXED
    width = pieces * LANES

    def kernel(scales_ref, packed_ref, crossed_ref, high_ref, low_ref, mean_ref, gram_ref, drive_ref, columns):
        for source in range(ring):
            for strip in range(strips):
                lanes = slice(strip * LANES, (strip + 1) * LANES)
                skip = strip if strip < pieces else strip + pieces
                own = source * depth + skip * rows
                other = (source * strips + strip) * rows
                at = HALVES * source * rows
                columns[at : at + rows, lanes] = packed_ref[own : own + rows, :]
                columns[at + rows : at + HALVES * rows, lanes] = crossed_ref[other : other + rows, :]
        scales = scales_ref[...]
        made = [
            scale(columns[:, width + which * LANES : width + (which + 1) * LANES], scales, slots - FIXED + which, slots)
            for which in range(FIXED)
        ]
        gram_ref[...] = gram([piece for piece, share in made])
        drive_ref[...] = sum(share for piece, share in made)
        ens = columns[:, 0:width]
        ens_mean = jnp.mean(ens, axis=0, keepdims=True)
        high_ref[...], low_ref[...] = parts(ens - ens_mean)
        mean_ref[...] = jnp.broadcast_to(ens_mean, mean_ref.shape)

    return pl.pallas_call(
        kernel,
        out_shape=(
            pltpu.VMEM((members, width), BF16),
            pltpu.VMEM((members, width), BF16),
            pltpu.VMEM((TILE, width), F32),
            pltpu.VMEM((members, members), F32),
            pltpu.VMEM((members, LANES), F32),
        ),
        in_specs=whole(3),
        out_specs=tuple(whole(5)),
        scratch_shapes=[pltpu.VMEM((members, strips * LANES), F32)],
        name="prepare",
    )(*near(scales, packed, crossed))


def analyse(obs, scales, prepared, rows):
    members, _ = obs.shape
    slots = scales.shape[0] // 2
    groups = members // rows
    width = prepared[0].shape[1]

    def kernel(obs_ref, scales_ref, high_ref, low_ref, mean_ref, gram_ref, drive_ref, out_ref):
        half = lax.axis_index("half")
        scales = scales_ref[...]
        made = [
            scale(obs_ref[:, slot * LANES : (slot + 1) * LANES], scales, slot, slots) for slot in range(slots - FIXED)
        ]
        drive = drive_ref[...] + sum(share for piece, share in made)
        gram_matrix = gram_ref[...] + gram([piece for piece, share in made])
        drive = jnp.sum(drive, axis=1, keepdims=True)
        identity = (
            lax.broadcasted_iota(I32, (members, members), 0) == lax.broadcasted_iota(I32, (members, members), 1)
        ).astype(F32)
        system = identity + gram_matrix / (members - 1.0)
        trace_sum = jnp.sum(system * identity, keepdims=True)
        iterate_y = system / trace_sum
        half_three = 1.5 * identity
        factor = half_three - 0.5 * iterate_y
        y_parts = parts(iterate_y)
        z_parts = parts(factor)
        y_parts = parts(product(y_parts, z_parts))
        for repeat in range(1, NEWTON):
            factor = parts(half_three - 0.5 * product(z_parts, y_parts))
            if repeat < NEWTON - 1:
                iterate_y = product(y_parts, factor)
            iterate_z = product(factor, z_parts)
            if repeat < NEWTON - 1:
                y_parts = parts(iterate_y)
                z_parts = parts(iterate_z)
        root = iterate_z / jnp.sqrt(trace_sum)
        half_step = jnp.sum(root * drive, axis=0, keepdims=True)
        mean_weights = jnp.sum(root * half_step, axis=1, keepdims=True) / (members - 1.0)
        anomalies = (high_ref[...], low_ref[...])
        spread = anomalies[0].astype(F32) + anomalies[1].astype(F32)
        shift = mean_ref[0:1, :] + jnp.sum(mean_weights * spread, axis=0, keepdims=True)
        updated = product(parts(root), anomalies) + shift
        for chunk in range(groups):
            group = chunk // HALVES * HALVES + (half ^ (chunk % HALVES))
            at = pl.multiple_of(group * rows, TILE)
            out_ref[pl.ds(at, rows), :] = updated[chunk * rows : (chunk + 1) * rows, :]

    return pl.pallas_call(
        kernel,
        out_shape=pltpu.VMEM((members, width), F32),
        in_specs=whole(7),
        out_specs=pl.BlockSpec(memory_space=pltpu.VMEM),
        name="analyse",
    )(*near(obs, scales, *prepared))


def on_device(ensemble, obs_pert, innovation, block_list, loc_weights):
    regions = lax.axis_size("reg")
    rows, own_obs = obs_pert.shape
    weights = loc_weights.reshape(loc_weights.shape[1:])

    partner = lax.ppermute(obs_pert, "half", [(0, 1), (1, 0)])
    packed = pack(ensemble, obs_pert, block_list)
    packed = lax.all_to_all(packed, "ring", split_axis=0, concat_axis=0, tiled=True)
    table = jnp.concatenate([obs_pert, partner, innovation.reshape(1, own_obs)], axis=0)
    swaps = [[(i + a, i + 1 - a) for i in range(first, regions - 1, 2) for a in (0, 1)] for first in (0, 1)]
    far_side = lax.ppermute(table, "reg", swaps[1])
    near_side = lax.ppermute(table, "reg", swaps[0])
    chosen, scales = select(packed, block_list.shape[1], weights, table, near_side, far_side)
    obs = lax.all_to_all(chosen, "ring", split_axis=0, concat_axis=0, tiled=True)
    ring = lax.axis_size("ring")
    chunks = packed.reshape(ring, -1, LANES)
    part = ensemble.shape[1] // (HALVES * ring) // LANES * rows
    crossed = lax.ppermute(chunks[:, part : chunks.shape[1] - TILE, :].reshape(-1, LANES), "half", [(0, 1), (1, 0)])
    prepared = prepare(scales, packed, crossed, rows)
    updated = analyse(obs, scales, prepared, rows)
    sent = lax.all_to_all(updated, MEM[::-1], split_axis=0, concat_axis=0, tiled=True)
    sent = sent.reshape(ring, HALVES, rows // TILE, TILE, -1)
    return sent.transpose(2, 3, 1, 0, 4).reshape(rows, -1)


def solution(mesh):
    groups, regions = (mesh.shape[name] for name in ("mem", "reg"))
    fine = Mesh(mesh.devices.reshape(HALVES, groups // HALVES, regions), MEM + ("reg",))
    return jax.shard_map(
        on_device,
        mesh=fine,
        in_specs=(
            P(MEM, "reg"),
            P(MEM, "reg"),
            P("reg"),
            P(("reg",) + MEM, None),
            P(("reg",) + MEM, None, None),
        ),
        out_specs=P(MEM, "reg"),
        check_vma=False,
    )
```

profile of v0, /device:TPU:68, one launch (start us, length us, event | category | flops | bytes accessed | tf_op | source)
XLA Modules:
  0.0 94.7 jit_solution(6342374901246422762)
XLA Ops:
  0.0 1.8 %pack.1 = f32[832,128]{1,0:T(8,128)} custom-call(f32[16,4096]{1,0:T(8,128)} %ens_ref.1, f32[16,1024]{1,0:T(8,128)} %obs_ref.1, s32[1,8]{1,0:T(1,128)} %list_ref.1), custom_call_target="tpu_custom_call" | custom-call | tf_op jit(solution)/shard_map/pack/pallas_call | solution.py:54
  1.8 0.0 copy-start.1
  1.8 0.0 copy-start.2
  1.8 7.2 %all-to-all-start = ((f32[8,104,128]{2,1,0:T(8,128)}), f32[8,104,128]{2,1,0:T(8,128)S(1)}, u32[]{:S(2)}, u32[]{:S(2)}) async-start(f32[8,104,128]{2,1,0:T(8,128)} %bitcast), calls=%async_computation | async-start | bytes 851968 | tf_op jit(solution)/shard_map/all_to_all | solution.py:287
  9.0 0.0 copy-done.1
  9.0 10.0 %collective-permute-start = (f32[16,1024]{1,0:T(8,128)S(1)}, f32[16,1024]{1,0:T(8,128)S(1)}, u32[]{:S(2)}, u32[]{:S(2)}) collective-permute-start(f32[16,1024]{1,0:T(8,128)S(1)} %copy-done.1), channel_id=1, source_target_pairs={{0,256},{256,0},{1,257},{257,1},{2,258},{258,2},{3,259},{259,3},{4... | collective-permute-start | bytes 196616 | tf_op jit(solution)/shard_map/ppermute | solution.py:285
  19.1 2.5 %collective-permute-done = f32[16,1024]{1,0:T(8,128)S(1)} collective-permute-done((f32[16,1024]{1,0:T(8,128)S(1)}, f32[16,1024]{1,0:T(8,128)S(1)}, u32[]{:S(2)}, u32[]{:S(2)}) %collective-permute-start) | collective-permute-done | bytes 65568 | tf_op jit(solution)/shard_map/ppermute | solution.py:285
  21.6 0.0 copy-done.2
  21.6 0.0 copy-start
  21.6 1.9 %collective-permute-start.1 = (f32[33,1024]{1,0:T(8,128)S(1)}, f32[33,1024]{1,0:T(8,128)S(1)}, u32[]{:S(2)}, u32[]{:S(2)}) collective-permute-start(f32[33,1024]{1,0:T(8,128)S(1)} %pad_maximum_fusion.own_ref), channel_id=1, source_target_pairs={{0,1},{1,0},{2,3},{3,2},{4,5},{5,4},{6,7},{7,6},{8,9},{9,8},{10,11... | collective-permute-start | bytes 405512 | tf_op jit(solution)/shard_map/ppermute | solution.py:291
  23.5 2.8 %collective-permute-start.2 = (f32[33,1024]{1,0:T(8,128)S(1)}, f32[33,1024]{1,0:T(8,128)S(1)}, u32[]{:S(2)}, u32[]{:S(2)}) collective-permute-start(f32[33,1024]{1,0:T(8,128)S(1)} %pad_maximum_fusion.own_ref), channel_id=1, source_target_pairs={{1,2},{2,1},{3,4},{4,3},{5,6},{6,5},{7,8},{8,7},{9,10},{10,9},{11,... | collective-permute-start | bytes 405512 | tf_op jit(solution)/shard_map/ppermute | solution.py:290
  26.4 0.0 collective-permute-done.1.near_ref
  26.4 3.8 %collective-permute-done.2.far_ref = f32[33,1024]{1,0:T(8,128)S(1)} collective-permute-done((f32[33,1024]{1,0:T(8,128)S(1)}, f32[33,1024]{1,0:T(8,128)S(1)}, u32[]{:S(2)}, u32[]{:S(2)}) %collective-permute-start.2) | collective-permute-done | bytes 135200 | tf_op jit(solution)/shard_map/ppermute | solution.py:290
  30.1 0.0 all-to-all-done
  30.2 0.0 copy-done
  30.2 1.6 %select.1 = (f32[256,768]{1,0:T(8,128)}, f32[16,128]{1,0:T(8,128)S(1)}) custom-call(f32[832,128]{1,0:T(8,128)S(1)} %bitcast.12, f32[8,128]{1,0:T(8,128)S(1)} %bitcast.16, f32[33,1024]{1,0:T(8,128)S(1)} %pad_maximum_fusion.own_ref, f32[33,1024]{1,0:T(8,128)S(1)} %collective-permute-done.1.near_ref, f32[33,1024]{1,0:T(8,128)S(1)} %collective-permute-done.2.far_ref), custom_call_target="tpu_custom_call" | custom-call | tf_op jit(solution)/shard_map/select/pallas_call | solution.py:122
  31.8 7.8 %all-to-all-start.1 = ((f32[8,32,768]{2,1,0:T(8,128)}), f32[8,32,768]{2,1,0:T(8,128)S(1)}, u32[]{:S(2)}, u32[]{:S(2)}) async-start(f32[8,32,768]{2,1,0:T(8,128)} %bitcast.18), calls=%async_computation.1 | async-start | bytes 1572864 | tf_op jit(solution)/shard_map/all_to_all | solution.py:293
  39.6 7.6 %collective-permute-start.3 = (f32[512,128]{1,0:T(8,128)S(1)}, f32[512,128]{1,0:T(8,128)S(1)}, u32[]{:S(2)}, u32[]{:S(2)}) collective-permute-start(f32[512,128]{1,0:T(8,128)S(1)} %bitcast.19), channel_id=1, source_target_pairs={{0,256},{256,0},{1,257},{257,1},{2,258},{258,2},{3,259},{259,3},{4... | collective-permute-start | bytes 786440 | tf_op jit(solution)/shard_map/ppermute | solution.py:297
  47.3 12.2 %collective-permute-done.3.crossed_ref = f32[512,128]{1,0:T(8,128)S(1)} collective-permute-done((f32[512,128]{1,0:T(8,128)S(1)}, f32[512,128]{1,0:T(8,128)S(1)}, u32[]{:S(2)}, u32[]{:S(2)}) %collective-permute-start.3) | collective-permute-done | bytes 262176 | tf_op jit(solution)/shard_map/ppermute | solution.py:297
  59.4 0.4 prepare.1
  59.8 4.2 %all-to-all-done.1 = f32[8,32,768]{2,1,0:T(8,128)S(1)} async-done(((f32[8,32,768]{2,1,0:T(8,128)}), f32[8,32,768]{2,1,0:T(8,128)S(1)}, u32[]{:S(2)}, u32[]{:S(2)}) %all-to-all-start.1) | async-done | bytes 786464 | tf_op jit(solution)/shard_map/all_to_all | solution.py:293
  64.1 5.1 %analyse.1 = f32[256,256]{1,0:T(8,128)S(1)} custom-call(f32[256,768]{1,0:T(8,128)S(1)} %bitcast.14, f32[16,128]{1,0:T(8,128)S(1)} %get-tuple-element.13.scales_ref, bf16[256,256]{1,0:T(8,128)(2,1)S(1)} %get-tuple-element.14.high_ref, bf16[256,256]{1,0:T(8,128)(2,1)S(1)} %get-tuple-element.15.low_ref, f32[8,256]{1,0:T(8,128)S(1)} %get-tuple-element.16.mean_ref, ...), custom_call_target="tpu_custom_call" | custom-call | tf_op jit(solution)/shard_map/analyse/pallas_call | solution.py:271
  69.2 24.8 %all_to_all.31 = f32[16,16,256]{2,1,0:T(8,128)S(1)} all-to-all(f32[16,16,256]{2,1,0:T(8,128)S(1)} %bitcast.15), channel_id=1, replica_groups=mesh['half'=2,'ring'=8,'reg'=32] {'ring','half'}, dimensions={0} | all-to-all | bytes 524288 | tf_op jit(solution)/shard_map/all_to_all | solution.py:300
  93.9 0.7 copy.6
  (2 shorter events, 0.0 us)
Async XLA Ops:
  1.8 7.2 %copy-start.1 = (f32[16,1024]{1,0:T(8,128)S(1)}, f32[16,1024]{1,0:T(8,128)}, u32[]{:S(2)}) copy-start(f32[16,1024]{1,0:T(8,128)} %obs_ref.1) | copy-start | bytes 196612
  1.8 19.8 %copy-start.2 = (f32[1024]{0:T(1024)S(1)}, f32[1024]{0:T(1024)}, u32[]{:S(2)}) copy-start(f32[1024]{0:T(1024)} %param.7) | copy-start | bytes 12292
  1.8 28.4 %all-to-all-start = ((f32[8,104,128]{2,1,0:T(8,128)}), f32[8,104,128]{2,1,0:T(8,128)S(1)}, u32[]{:S(2)}, u32[]{:S(2)}) async-start(f32[8,104,128]{2,1,0:T(8,128)} %bitcast), calls=%async_computation | async-start | bytes 851968 | tf_op jit(solution)/shard_map/all_to_all | solution.py:287
  9.0 12.5 %collective-permute-start = (f32[16,1024]{1,0:T(8,128)S(1)}, f32[16,1024]{1,0:T(8,128)S(1)}, u32[]{:S(2)}, u32[]{:S(2)}) collective-permute-start(f32[16,1024]{1,0:T(8,128)S(1)} %copy-done.1), channel_id=1, source_target_pairs={{0,256},{256,0},{1,257},{257,1},{2,258},{258,2},{3,259},{259,3},{4... | collective-permute-start | bytes 196616 | tf_op jit(solution)/shard_map/ppermute | solution.py:285
  21.6 8.6 %copy-start = (f32[1,8,128]{2,1,0:T(8,128)S(1)}, f32[1,8,128]{2,1,0:T(8,128)}, u32[]{:S(2)}) copy-start(f32[1,8,128]{2,1,0:T(8,128)} %param.9) | copy-start | bytes 12292
  21.6 4.8 %collective-permute-start.1 = (f32[33,1024]{1,0:T(8,128)S(1)}, f32[33,1024]{1,0:T(8,128)S(1)}, u32[]{:S(2)}, u32[]{:S(2)}) collective-permute-start(f32[33,1024]{1,0:T(8,128)S(1)} %pad_maximum_fusion.own_ref), channel_id=1, source_target_pairs={{0,1},{1,0},{2,3},{3,2},{4,5},{5,4},{6,7},{7,6},{8,9},{9,8},{10,11... | collective-permute-start | bytes 405512 | tf_op jit(solution)/shard_map/ppermute | solution.py:291
  23.5 6.6 %collective-permute-start.2 = (f32[33,1024]{1,0:T(8,128)S(1)}, f32[33,1024]{1,0:T(8,128)S(1)}, u32[]{:S(2)}, u32[]{:S(2)}) collective-permute-start(f32[33,1024]{1,0:T(8,128)S(1)} %pad_maximum_fusion.own_ref), channel_id=1, source_target_pairs={{1,2},{2,1},{3,4},{4,3},{5,6},{6,5},{7,8},{8,7},{9,10},{10,9},{11,... | collective-permute-start | bytes 405512 | tf_op jit(solution)/shard_map/ppermute | solution.py:290
  31.8 32.3 %all-to-all-start.1 = ((f32[8,32,768]{2,1,0:T(8,128)}), f32[8,32,768]{2,1,0:T(8,128)S(1)}, u32[]{:S(2)}, u32[]{:S(2)}) async-start(f32[8,32,768]{2,1,0:T(8,128)} %bitcast.18), calls=%async_computation.1 | async-start | bytes 1572864 | tf_op jit(solution)/shard_map/all_to_all | solution.py:293
  39.6 19.8 %collective-permute-start.3 = (f32[512,128]{1,0:T(8,128)S(1)}, f32[512,128]{1,0:T(8,128)S(1)}, u32[]{:S(2)}, u32[]{:S(2)}) collective-permute-start(f32[512,128]{1,0:T(8,128)S(1)} %bitcast.19), channel_id=1, source_target_pairs={{0,256},{256,0},{1,257},{257,1},{2,258},{258,2},{3,259},{259,3},{4... | collective-permute-start | bytes 786440 | tf_op jit(solution)/shard_map/ppermute | solution.py:297
where the time goes:
time: 95.1 us; the launch traced here: 94.7 us
  starting transfers between devices  37.5 us (39%)
  blocking collectives  24.8 us (26%)
  waiting for transfers between devices  22.7 us (24%)
  Pallas kernels  8.89 us (9%)
    all_to_all x1, blocking collectives, on_device(): lax.all_to_all(updated, MEM[::-1], split_axis=0, concat_axis=0, tiled=True)  24.8 us
    ppermute x1, waiting for transfers between devices, on_device(): lax.ppermute(chunks[:, part:chunks.shape[1] - TILE, :].reshape(-1, LANES)...  12.2 us
    ppermute x1, starting transfers between devices, on_device(): partner = lax.ppermute(obs_pert, 'half', [(0, 1), (1, 0)])  10 us
    all_to_all x1, starting transfers between devices, on_device(): lax.all_to_all(chosen, 'ring', split_axis=0, concat_axis=0, tiled=True)  7.83 us
    ppermute x1, starting transfers between devices, on_device(): lax.ppermute(chunks[:, part:chunks.shape[1] - TILE, :].reshape(-1, LANES)...  7.64 us
    all_to_all x1, starting transfers between devices, on_device(): lax.all_to_all(packed, 'ring', split_axis=0, concat_axis=0, tiled=True)  7.23 us
    pallas_call x1, Pallas kernels, analyse(): pl.pallas_call(kernel, out_shape=pltpu.VMEM((members, width), F32), in_sp...  5.11 us
    all_to_all x1, waiting for transfers between devices, on_device(): lax.all_to_all(chosen, 'ring', split_axis=0, concat_axis=0, tiled=True)  4.23 us
  transfers between devices with their start and end apart: 6, of which 4 were waited for; matrix products, arithmetic and copies ran while one was open for 0% of the time, Pallas kernels for 0%

commit v1 on v0

--- a/solution.py
+++ b/solution.py
@@ -226,6 +226,7 @@
     members, _ = obs.shape
     slots = scales.shape[0] // 2
     groups = members // rows
+    ring = groups // HALVES
     width = prepared[0].shape[1]
 
     def kernel(obs_ref, scales_ref, high_ref, low_ref, mean_ref, gram_ref, drive_ref, out_ref):
@@ -264,7 +265,7 @@
         shift = mean_ref[0:1, :] + jnp.sum(mean_weights * spread, axis=0, keepdims=True)
         updated = product(parts(root), anomalies) + shift
         for chunk in range(groups):
-            group = chunk // HALVES * HALVES + (half ^ (chunk % HALVES))
+            group = (1 - (half ^ (chunk % HALVES))) * ring + chunk // HALVES
             at = pl.multiple_of(group * rows, TILE)
             out_ref[pl.ds(at, rows), :] = updated[chunk * rows : (chunk + 1) * rows, :]
 
@@ -275,6 +276,31 @@
         out_specs=pl.BlockSpec(memory_space=pltpu.VMEM),
         name="analyse",
     )(*near(obs, scales, *prepared))
+
+
+def place(sent, order):
+    groups = len(order)
+    rows = sent.shape[0] // groups
+    width = sent.shape[1]
+
+    def kernel(sent_ref, out_ref, sems):
+        copies = []
+        for at, patch in enumerate(order):
+            source = sent_ref.at[at * rows : (at + 1) * rows]
+            target = out_ref.at[:, patch * width : (patch + 1) * width]
+            copies.append(pltpu.make_async_copy(source, target, sems.at[at]))
+            copies[-1].start()
+        for copy in copies:
+            copy.wait()
+
+    return pl.pallas_call(
+        kernel,
+        out_shape=jax.ShapeDtypeStruct((rows, groups * width), F32),
+        in_specs=whole(1),
+        out_specs=pl.BlockSpec(memory_space=pl.ANY),
+        scratch_shapes=[pltpu.SemaphoreType.DMA((groups,))],
+        name="place",
+    )(*near(sent))
 
 
 def on_device(ensemble, obs_pert, innovation, block_list, loc_weights):
@@ -297,9 +323,11 @@
     crossed = lax.ppermute(chunks[:, part : chunks.shape[1] - TILE, :].reshape(-1, LANES), "half", [(0, 1), (1, 0)])
     prepared = prepare(scales, packed, crossed, rows)
     updated = analyse(obs, scales, prepared, rows)
-    sent = lax.all_to_all(updated, MEM[::-1], split_axis=0, concat_axis=0, tiled=True)
-    sent = sent.reshape(ring, HALVES, rows // TILE, TILE, -1)
-    return sent.transpose(2, 3, 1, 0, 4).reshape(rows, -1)
+    order = [(i + ring) % (HALVES * ring) for i in range(HALVES * ring)]
+    sent = lax.all_to_all(
+        updated, MEM, split_axis=0, concat_axis=0, tiled=True, axis_index_groups=[order]
+    )
+    return place(sent, order)
 
 
 def solution(mesh):

time: 95.1 us -> 89.6 us (0.942)
  the two profiles are of different devices: /device:TPU:68 before, /device:TPU:76 now
where the time goes in v1:
time: 89.6 us; the launch traced here: 89.2 us
  starting transfers between devices  36.4 us (41%)
  waiting for transfers between devices  21.8 us (24%)
  blocking collectives  21 us (23%)
  Pallas kernels  9.72 us (11%)
    all_to_all x1, blocking collectives, on_device(): lax.all_to_all(updated, MEM, split_axis=0, concat_axis=0, tiled=True, axi...  21 us
    ppermute x1, waiting for transfers between devices, on_device(): lax.ppermute(chunks[:, part:chunks.shape[1] - TILE, :].reshape(-1, LANES)...  12.4 us
    ppermute x1, starting transfers between devices, on_device(): partner = lax.ppermute(obs_pert, 'half', [(0, 1), (1, 0)])  10 us
    all_to_all x1, starting transfers between devices, on_device(): lax.all_to_all(packed, 'ring', split_axis=0, concat_axis=0, tiled=True)  7.68 us
    ppermute x1, starting transfers between devices, on_device(): lax.ppermute(chunks[:, part:chunks.shape[1] - TILE, :].reshape(-1, LANES)...  7.64 us
    all_to_all x1, starting transfers between devices, on_device(): lax.all_to_all(chosen, 'ring', split_axis=0, concat_axis=0, tiled=True)  7.22 us
    pallas_call x1, Pallas kernels, analyse(): pl.pallas_call(kernel, out_shape=pltpu.VMEM((members, width), F32), in_sp...  5.12 us
    ppermute x1, waiting for transfers between devices, on_device(): far_side = lax.ppermute(table, 'reg', swaps[1])  4.73 us
  transfers between devices with their start and end apart: 6, of which 4 were waited for; matrix products, arithmetic and copies ran while one was open for 0% of the time, Pallas kernels for 0%

profile of v1, /device:TPU:76, one launch (start us, length us, event | category | flops | bytes accessed | tf_op | source)
XLA Modules:
  0.0 89.2 jit_solution(13836432157583454246)
XLA Ops:
  0.0 1.8 %pack.1 = f32[832,128]{1,0:T(8,128)} custom-call(f32[16,4096]{1,0:T(8,128)} %ens_ref.1, f32[16,1024]{1,0:T(8,128)} %obs_ref.1, s32[1,8]{1,0:T(1,128)} %list_ref.1), custom_call_target="tpu_custom_call" | custom-call | tf_op jit(solution)/shard_map/pack/pallas_call | solution.py:54
  1.8 0.0 copy-start.1
  1.8 0.0 copy-start.2
  1.8 7.7 %all-to-all-start = ((f32[8,104,128]{2,1,0:T(8,128)}), f32[8,104,128]{2,1,0:T(8,128)S(1)}, u32[]{:S(2)}, u32[]{:S(2)}) async-start(f32[8,104,128]{2,1,0:T(8,128)} %bitcast), calls=%async_computation | async-start | bytes 851968 | tf_op jit(solution)/shard_map/all_to_all | solution.py:313
  9.5 0.0 copy-done.1
  9.5 10.0 %collective-permute-start = (f32[16,1024]{1,0:T(8,128)S(1)}, f32[16,1024]{1,0:T(8,128)S(1)}, u32[]{:S(2)}, u32[]{:S(2)}) collective-permute-start(f32[16,1024]{1,0:T(8,128)S(1)} %copy-done.1), channel_id=1, source_target_pairs={{0,256},{256,0},{1,257},{257,1},{2,258},{258,2},{3,259},{259,3},{4... | collective-permute-start | bytes 196616 | tf_op jit(solution)/shard_map/ppermute | solution.py:311
  19.5 3.0 %collective-permute-done = f32[16,1024]{1,0:T(8,128)S(1)} collective-permute-done((f32[16,1024]{1,0:T(8,128)S(1)}, f32[16,1024]{1,0:T(8,128)S(1)}, u32[]{:S(2)}, u32[]{:S(2)}) %collective-permute-start) | collective-permute-done | bytes 65568 | tf_op jit(solution)/shard_map/ppermute | solution.py:311
  22.5 0.0 copy-done.2
  22.5 0.0 copy-start
  22.5 1.9 %collective-permute-start.1 = (f32[33,1024]{1,0:T(8,128)S(1)}, f32[33,1024]{1,0:T(8,128)S(1)}, u32[]{:S(2)}, u32[]{:S(2)}) collective-permute-start(f32[33,1024]{1,0:T(8,128)S(1)} %pad_maximum_fusion.own_ref), channel_id=1, source_target_pairs={{0,1},{1,0},{2,3},{3,2},{4,5},{5,4},{6,7},{7,6},{8,9},{9,8},{10,11... | collective-permute-start | bytes 405512 | tf_op jit(solution)/shard_map/ppermute | solution.py:317
  24.5 2.0 %collective-permute-start.2 = (f32[33,1024]{1,0:T(8,128)S(1)}, f32[33,1024]{1,0:T(8,128)S(1)}, u32[]{:S(2)}, u32[]{:S(2)}) collective-permute-start(f32[33,1024]{1,0:T(8,128)S(1)} %pad_maximum_fusion.own_ref), channel_id=1, source_target_pairs={{1,2},{2,1},{3,4},{4,3},{5,6},{6,5},{7,8},{8,7},{9,10},{10,9},{11,... | collective-permute-start | bytes 405512 | tf_op jit(solution)/shard_map/ppermute | solution.py:316
  26.5 0.0 collective-permute-done.1.near_ref
  26.5 4.7 %collective-permute-done.2.far_ref = f32[33,1024]{1,0:T(8,128)S(1)} collective-permute-done((f32[33,1024]{1,0:T(8,128)S(1)}, f32[33,1024]{1,0:T(8,128)S(1)}, u32[]{:S(2)}, u32[]{:S(2)}) %collective-permute-start.2) | collective-permute-done | bytes 135200 | tf_op jit(solution)/shard_map/ppermute | solution.py:316
  31.2 0.0 all-to-all-done
  31.2 0.0 copy-done
  31.2 1.6 %select.1 = (f32[256,768]{1,0:T(8,128)}, f32[16,128]{1,0:T(8,128)S(1)}) custom-call(f32[832,128]{1,0:T(8,128)S(1)} %bitcast.9, f32[8,128]{1,0:T(8,128)S(1)} %bitcast.14, f32[33,1024]{1,0:T(8,128)S(1)} %pad_maximum_fusion.own_ref, f32[33,1024]{1,0:T(8,128)S(1)} %collective-permute-done.1.near_ref, f32[33,1024]{1,0:T(8,128)S(1)} %collective-permute-done.2.far_ref), custom_call_target="tpu_custom_call" | custom-call | tf_op jit(solution)/shard_map/select/pallas_call | solution.py:122
  32.8 7.2 %all-to-all-start.1 = ((f32[8,32,768]{2,1,0:T(8,128)}), f32[8,32,768]{2,1,0:T(8,128)S(1)}, u32[]{:S(2)}, u32[]{:S(2)}) async-start(f32[8,32,768]{2,1,0:T(8,128)} %bitcast.15), calls=%async_computation.1 | async-start | bytes 1572864 | tf_op jit(solution)/shard_map/all_to_all | solution.py:319
  40.1 7.6 %collective-permute-start.3 = (f32[512,128]{1,0:T(8,128)S(1)}, f32[512,128]{1,0:T(8,128)S(1)}, u32[]{:S(2)}, u32[]{:S(2)}) collective-permute-start(f32[512,128]{1,0:T(8,128)S(1)} %bitcast.16), channel_id=1, source_target_pairs={{0,256},{256,0},{1,257},{257,1},{2,258},{258,2},{3,259},{259,3},{4... | collective-permute-start | bytes 786440 | tf_op jit(solution)/shard_map/ppermute | solution.py:323
  47.7 12.4 %collective-permute-done.3.crossed_ref = f32[512,128]{1,0:T(8,128)S(1)} collective-permute-done((f32[512,128]{1,0:T(8,128)S(1)}, f32[512,128]{1,0:T(8,128)S(1)}, u32[]{:S(2)}, u32[]{:S(2)}) %collective-permute-start.3) | collective-permute-done | bytes 262176 | tf_op jit(solution)/shard_map/ppermute | solution.py:323
  60.2 0.4 prepare.1
  60.5 1.6 %all-to-all-done.1 = f32[8,32,768]{2,1,0:T(8,128)S(1)} async-done(((f32[8,32,768]{2,1,0:T(8,128)}), f32[8,32,768]{2,1,0:T(8,128)S(1)}, u32[]{:S(2)}, u32[]{:S(2)}) %all-to-all-start.1) | async-done | bytes 786464 | tf_op jit(solution)/shard_map/all_to_all | solution.py:319
  62.2 5.1 %analyse.1 = f32[256,256]{1,0:T(8,128)S(1)} custom-call(f32[256,768]{1,0:T(8,128)S(1)} %bitcast.11, f32[16,128]{1,0:T(8,128)S(1)} %get-tuple-element.13.scales_ref, bf16[256,256]{1,0:T(8,128)(2,1)S(1)} %get-tuple-element.14.high_ref, bf16[256,256]{1,0:T(8,128)(2,1)S(1)} %get-tuple-element.15.low_ref, f32[8,256]{1,0:T(8,128)S(1)} %get-tuple-element.16.mean_ref, ...), custom_call_target="tpu_custom_call" | custom-call | tf_op jit(solution)/shard_map/analyse/pallas_call | solution.py:272
  67.3 21.0 %all_to_all.33 = f32[16,16,256]{2,1,0:T(8,128)S(1)} all-to-all(f32[16,16,256]{2,1,0:T(8,128)S(1)} %bitcast.13), channel_id=1, replica_groups={{256,288,320,352,384,416,448,480,0,32,64,96,128,160,192,224},{257,289,3..., dimensions={0} | all-to-all | bytes 524288 | tf_op jit(solution)/shard_map/all_to_all | solution.py:327
  88.3 0.8 place.1
  (2 shorter events, 0.0 us)
Async XLA Ops:
  1.8 7.7 %copy-start.1 = (f32[16,1024]{1,0:T(8,128)S(1)}, f32[16,1024]{1,0:T(8,128)}, u32[]{:S(2)}) copy-start(f32[16,1024]{1,0:T(8,128)} %obs_ref.1) | copy-start | bytes 196612
  1.8 20.7 %copy-start.2 = (f32[1024]{0:T(1024)S(1)}, f32[1024]{0:T(1024)}, u32[]{:S(2)}) copy-start(f32[1024]{0:T(1024)} %param.7) | copy-start | bytes 12292
  1.8 29.4 %all-to-all-start = ((f32[8,104,128]{2,1,0:T(8,128)}), f32[8,104,128]{2,1,0:T(8,128)S(1)}, u32[]{:S(2)}, u32[]{:S(2)}) async-start(f32[8,104,128]{2,1,0:T(8,128)} %bitcast), calls=%async_computation | async-start | bytes 851968 | tf_op jit(solution)/shard_map/all_to_all | solution.py:313
  9.5 13.0 %collective-permute-start = (f32[16,1024]{1,0:T(8,128)S(1)}, f32[16,1024]{1,0:T(8,128)S(1)}, u32[]{:S(2)}, u32[]{:S(2)}) collective-permute-start(f32[16,1024]{1,0:T(8,128)S(1)} %copy-done.1), channel_id=1, source_target_pairs={{0,256},{256,0},{1,257},{257,1},{2,258},{258,2},{3,259},{259,3},{4... | collective-permute-start | bytes 196616 | tf_op jit(solution)/shard_map/ppermute | solution.py:311
  22.5 8.7 %copy-start = (f32[1,8,128]{2,1,0:T(8,128)S(1)}, f32[1,8,128]{2,1,0:T(8,128)}, u32[]{:S(2)}) copy-start(f32[1,8,128]{2,1,0:T(8,128)} %param.9) | copy-start | bytes 12292
  22.5 3.9 %collective-permute-start.1 = (f32[33,1024]{1,0:T(8,128)S(1)}, f32[33,1024]{1,0:T(8,128)S(1)}, u32[]{:S(2)}, u32[]{:S(2)}) collective-permute-start(f32[33,1024]{1,0:T(8,128)S(1)} %pad_maximum_fusion.own_ref), channel_id=1, source_target_pairs={{0,1},{1,0},{2,3},{3,2},{4,5},{5,4},{6,7},{7,6},{8,9},{9,8},{10,11... | collective-permute-start | bytes 405512 | tf_op jit(solution)/shard_map/ppermute | solution.py:317
  24.5 6.7 %collective-permute-start.2 = (f32[33,1024]{1,0:T(8,128)S(1)}, f32[33,1024]{1,0:T(8,128)S(1)}, u32[]{:S(2)}, u32[]{:S(2)}) collective-permute-start(f32[33,1024]{1,0:T(8,128)S(1)} %pad_maximum_fusion.own_ref), channel_id=1, source_target_pairs={{1,2},{2,1},{3,4},{4,3},{5,6},{6,5},{7,8},{8,7},{9,10},{10,9},{11,... | collective-permute-start | bytes 405512 | tf_op jit(solution)/shard_map/ppermute | solution.py:316
  32.8 29.3 %all-to-all-start.1 = ((f32[8,32,768]{2,1,0:T(8,128)}), f32[8,32,768]{2,1,0:T(8,128)S(1)}, u32[]{:S(2)}, u32[]{:S(2)}) async-start(f32[8,32,768]{2,1,0:T(8,128)} %bitcast.15), calls=%async_computation.1 | async-start | bytes 1572864 | tf_op jit(solution)/shard_map/all_to_all | solution.py:319
  40.1 20.1 %collective-permute-start.3 = (f32[512,128]{1,0:T(8,128)S(1)}, f32[512,128]{1,0:T(8,128)S(1)}, u32[]{:S(2)}, u32[]{:S(2)}) collective-permute-start(f32[512,128]{1,0:T(8,128)S(1)} %bitcast.16), channel_id=1, source_target_pairs={{0,256},{256,0},{1,257},{257,1},{2,258},{258,2},{3,259},{259,3},{4... | collective-permute-start | bytes 786440 | tf_op jit(solution)/shard_map/ppermute | solution.py:323

commit v2 on v0

--- a/solution.py
+++ b/solution.py
@@ -226,6 +226,7 @@
     members, _ = obs.shape
     slots = scales.shape[0] // 2
     groups = members // rows
+    ring = groups // HALVES
     width = prepared[0].shape[1]
 
     def kernel(obs_ref, scales_ref, high_ref, low_ref, mean_ref, gram_ref, drive_ref, out_ref):
@@ -264,7 +265,7 @@
         shift = mean_ref[0:1, :] + jnp.sum(mean_weights * spread, axis=0, keepdims=True)
         updated = product(parts(root), anomalies) + shift
         for chunk in range(groups):
-            group = chunk // HALVES * HALVES + (half ^ (chunk % HALVES))
+            group = (half ^ (chunk % HALVES)) * ring + chunk // HALVES
             at = pl.multiple_of(group * rows, TILE)
             out_ref[pl.ds(at, rows), :] = updated[chunk * rows : (chunk + 1) * rows, :]
 
@@ -297,9 +298,8 @@
     crossed = lax.ppermute(chunks[:, part : chunks.shape[1] - TILE, :].reshape(-1, LANES), "half", [(0, 1), (1, 0)])
     prepared = prepare(scales, packed, crossed, rows)
     updated = analyse(obs, scales, prepared, rows)
-    sent = lax.all_to_all(updated, MEM[::-1], split_axis=0, concat_axis=0, tiled=True)
-    sent = sent.reshape(ring, HALVES, rows // TILE, TILE, -1)
-    return sent.transpose(2, 3, 1, 0, 4).reshape(rows, -1)
+    sent = lax.all_to_all(updated, MEM, split_axis=0, concat_axis=0, tiled=True)
+    return sent.reshape(sent.shape[0] // rows, rows, -1).transpose(1, 0, 2).reshape(rows, -1)
 
 
 def solution(mesh):

time: 95.1 us -> 93.5 us (0.983)
  the two profiles are of different devices: /device:TPU:68 before, /device:TPU:76 now
where the time goes in v2:
time: 93.5 us; the launch traced here: 93 us
  starting transfers between devices  36.4 us (39%)
  blocking collectives  25 us (27%)
  waiting for transfers between devices  21.8 us (23%)
  Pallas kernels  8.9 us (10%)
    all_to_all x1, blocking collectives, on_device(): sent = lax.all_to_all(updated, MEM, split_axis=0, concat_axis=0, tiled=True)  25 us
    ppermute x1, waiting for transfers between devices, on_device(): lax.ppermute(chunks[:, part:chunks.shape[1] - TILE, :].reshape(-1, LANES)...  12.4 us
    ppermute x1, starting transfers between devices, on_device(): partner = lax.ppermute(obs_pert, 'half', [(0, 1), (1, 0)])  10 us
    all_to_all x1, starting transfers between devices, on_device(): lax.all_to_all(packed, 'ring', split_axis=0, concat_axis=0, tiled=True)  7.68 us
    ppermute x1, starting transfers between devices, on_device(): lax.ppermute(chunks[:, part:chunks.shape[1] - TILE, :].reshape(-1, LANES)...  7.64 us
    all_to_all x1, starting transfers between devices, on_device(): lax.all_to_all(chosen, 'ring', split_axis=0, concat_axis=0, tiled=True)  7.22 us
    pallas_call x1, Pallas kernels, analyse(): pl.pallas_call(kernel, out_shape=pltpu.VMEM((members, width), F32), in_sp...  5.12 us
    ppermute x1, waiting for transfers between devices, on_device(): far_side = lax.ppermute(table, 'reg', swaps[1])  4.73 us
  transfers between devices with their start and end apart: 6, of which 4 were waited for; matrix products, arithmetic and copies ran while one was open for 0% of the time, Pallas kernels for 0%

profile of v2, /device:TPU:76, one launch (start us, length us, event | category | flops | bytes accessed | tf_op | source)
XLA Modules:
  0.0 93.0 jit_solution(16873474079247046250)
XLA Ops:
  0.0 1.8 %pack.1 = f32[832,128]{1,0:T(8,128)} custom-call(f32[16,4096]{1,0:T(8,128)} %ens_ref.1, f32[16,1024]{1,0:T(8,128)} %obs_ref.1, s32[1,8]{1,0:T(1,128)} %list_ref.1), custom_call_target="tpu_custom_call" | custom-call | tf_op jit(solution)/shard_map/pack/pallas_call | solution.py:54
  1.8 0.0 copy-start.1
  1.8 0.0 copy-start.2
  1.8 7.7 %all-to-all-start = ((f32[8,104,128]{2,1,0:T(8,128)}), f32[8,104,128]{2,1,0:T(8,128)S(1)}, u32[]{:S(2)}, u32[]{:S(2)}) async-start(f32[8,104,128]{2,1,0:T(8,128)} %bitcast), calls=%async_computation | async-start | bytes 851968 | tf_op jit(solution)/shard_map/all_to_all | solution.py:288
  9.5 0.0 copy-done.1
  9.5 10.0 %collective-permute-start = (f32[16,1024]{1,0:T(8,128)S(1)}, f32[16,1024]{1,0:T(8,128)S(1)}, u32[]{:S(2)}, u32[]{:S(2)}) collective-permute-start(f32[16,1024]{1,0:T(8,128)S(1)} %copy-done.1), channel_id=1, source_target_pairs={{0,256},{256,0},{1,257},{257,1},{2,258},{258,2},{3,259},{259,3},{4... | collective-permute-start | bytes 196616 | tf_op jit(solution)/shard_map/ppermute | solution.py:286
  19.5 3.0 %collective-permute-done = f32[16,1024]{1,0:T(8,128)S(1)} collective-permute-done((f32[16,1024]{1,0:T(8,128)S(1)}, f32[16,1024]{1,0:T(8,128)S(1)}, u32[]{:S(2)}, u32[]{:S(2)}) %collective-permute-start) | collective-permute-done | bytes 65568 | tf_op jit(solution)/shard_map/ppermute | solution.py:286
  22.5 0.0 copy-done.2
  22.5 0.0 copy-start
  22.5 1.9 %collective-permute-start.1 = (f32[33,1024]{1,0:T(8,128)S(1)}, f32[33,1024]{1,0:T(8,128)S(1)}, u32[]{:S(2)}, u32[]{:S(2)}) collective-permute-start(f32[33,1024]{1,0:T(8,128)S(1)} %pad_maximum_fusion.own_ref), channel_id=1, source_target_pairs={{0,1},{1,0},{2,3},{3,2},{4,5},{5,4},{6,7},{7,6},{8,9},{9,8},{10,11... | collective-permute-start | bytes 405512 | tf_op jit(solution)/shard_map/ppermute | solution.py:292
  24.5 2.0 %collective-permute-start.2 = (f32[33,1024]{1,0:T(8,128)S(1)}, f32[33,1024]{1,0:T(8,128)S(1)}, u32[]{:S(2)}, u32[]{:S(2)}) collective-permute-start(f32[33,1024]{1,0:T(8,128)S(1)} %pad_maximum_fusion.own_ref), channel_id=1, source_target_pairs={{1,2},{2,1},{3,4},{4,3},{5,6},{6,5},{7,8},{8,7},{9,10},{10,9},{11,... | collective-permute-start | bytes 405512 | tf_op jit(solution)/shard_map/ppermute | solution.py:291
  26.5 0.0 collective-permute-done.1.near_ref
  26.5 4.7 %collective-permute-done.2.far_ref = f32[33,1024]{1,0:T(8,128)S(1)} collective-permute-done((f32[33,1024]{1,0:T(8,128)S(1)}, f32[33,1024]{1,0:T(8,128)S(1)}, u32[]{:S(2)}, u32[]{:S(2)}) %collective-permute-start.2) | collective-permute-done | bytes 135200 | tf_op jit(solution)/shard_map/ppermute | solution.py:291
  31.2 0.0 all-to-all-done
  31.2 0.0 copy-done
  31.2 1.6 %select.1 = (f32[256,768]{1,0:T(8,128)}, f32[16,128]{1,0:T(8,128)S(1)}) custom-call(f32[832,128]{1,0:T(8,128)S(1)} %bitcast.11, f32[8,128]{1,0:T(8,128)S(1)} %bitcast.15, f32[33,1024]{1,0:T(8,128)S(1)} %pad_maximum_fusion.own_ref, f32[33,1024]{1,0:T(8,128)S(1)} %collective-permute-done.1.near_ref, f32[33,1024]{1,0:T(8,128)S(1)} %collective-permute-done.2.far_ref), custom_call_target="tpu_custom_call" | custom-call | tf_op jit(solution)/shard_map/select/pallas_call | solution.py:122
  32.8 7.2 %all-to-all-start.1 = ((f32[8,32,768]{2,1,0:T(8,128)}), f32[8,32,768]{2,1,0:T(8,128)S(1)}, u32[]{:S(2)}, u32[]{:S(2)}) async-start(f32[8,32,768]{2,1,0:T(8,128)} %bitcast.17), calls=%async_computation.1 | async-start | bytes 1572864 | tf_op jit(solution)/shard_map/all_to_all | solution.py:294
  40.1 7.6 %collective-permute-start.3 = (f32[512,128]{1,0:T(8,128)S(1)}, f32[512,128]{1,0:T(8,128)S(1)}, u32[]{:S(2)}, u32[]{:S(2)}) collective-permute-start(f32[512,128]{1,0:T(8,128)S(1)} %bitcast.18), channel_id=1, source_target_pairs={{0,256},{256,0},{1,257},{257,1},{2,258},{258,2},{3,259},{259,3},{4... | collective-permute-start | bytes 786440 | tf_op jit(solution)/shard_map/ppermute | solution.py:298
  47.7 12.4 %collective-permute-done.3.crossed_ref = f32[512,128]{1,0:T(8,128)S(1)} collective-permute-done((f32[512,128]{1,0:T(8,128)S(1)}, f32[512,128]{1,0:T(8,128)S(1)}, u32[]{:S(2)}, u32[]{:S(2)}) %collective-permute-start.3) | collective-permute-done | bytes 262176 | tf_op jit(solution)/shard_map/ppermute | solution.py:298
  60.2 0.4 prepare.1
  60.5 1.6 %all-to-all-done.1 = f32[8,32,768]{2,1,0:T(8,128)S(1)} async-done(((f32[8,32,768]{2,1,0:T(8,128)}), f32[8,32,768]{2,1,0:T(8,128)S(1)}, u32[]{:S(2)}, u32[]{:S(2)}) %all-to-all-start.1) | async-done | bytes 786464 | tf_op jit(solution)/shard_map/all_to_all | solution.py:294
  62.2 5.1 %analyse.1 = f32[256,256]{1,0:T(8,128)S(1)} custom-call(f32[256,768]{1,0:T(8,128)S(1)} %bitcast.13, f32[16,128]{1,0:T(8,128)S(1)} %get-tuple-element.13.scales_ref, bf16[256,256]{1,0:T(8,128)(2,1)S(1)} %get-tuple-element.14.high_ref, bf16[256,256]{1,0:T(8,128)(2,1)S(1)} %get-tuple-element.15.low_ref, f32[8,256]{1,0:T(8,128)S(1)} %get-tuple-element.16.mean_ref, ...), custom_call_target="tpu_custom_call" | custom-call | tf_op jit(solution)/shard_map/analyse/pallas_call | solution.py:272
  67.3 25.0 %all_to_all.31 = f32[16,16,256]{2,1,0:T(8,128)S(1)} all-to-all(f32[16,16,256]{2,1,0:T(8,128)S(1)} %bitcast.14), channel_id=1, replica_groups=mesh['half'=2,'ring'=8,'reg'=32] {'half','ring'}, dimensions={0} | all-to-all | bytes 524288 | tf_op jit(solution)/shard_map/all_to_all | solution.py:301
  92.3 0.7 copy.7
  (2 shorter events, 0.0 us)
Async XLA Ops:
  1.8 7.7 %copy-start.1 = (f32[16,1024]{1,0:T(8,128)S(1)}, f32[16,1024]{1,0:T(8,128)}, u32[]{:S(2)}) copy-start(f32[16,1024]{1,0:T(8,128)} %obs_ref.1) | copy-start | bytes 196612
  1.8 20.7 %copy-start.2 = (f32[1024]{0:T(1024)S(1)}, f32[1024]{0:T(1024)}, u32[]{:S(2)}) copy-start(f32[1024]{0:T(1024)} %param.7) | copy-start | bytes 12292
  1.8 29.4 %all-to-all-start = ((f32[8,104,128]{2,1,0:T(8,128)}), f32[8,104,128]{2,1,0:T(8,128)S(1)}, u32[]{:S(2)}, u32[]{:S(2)}) async-start(f32[8,104,128]{2,1,0:T(8,128)} %bitcast), calls=%async_computation | async-start | bytes 851968 | tf_op jit(solution)/shard_map/all_to_all | solution.py:288
  9.5 13.0 %collective-permute-start = (f32[16,1024]{1,0:T(8,128)S(1)}, f32[16,1024]{1,0:T(8,128)S(1)}, u32[]{:S(2)}, u32[]{:S(2)}) collective-permute-start(f32[16,1024]{1,0:T(8,128)S(1)} %copy-done.1), channel_id=1, source_target_pairs={{0,256},{256,0},{1,257},{257,1},{2,258},{258,2},{3,259},{259,3},{4... | collective-permute-start | bytes 196616 | tf_op jit(solution)/shard_map/ppermute | solution.py:286
  22.5 8.7 %copy-start = (f32[1,8,128]{2,1,0:T(8,128)S(1)}, f32[1,8,128]{2,1,0:T(8,128)}, u32[]{:S(2)}) copy-start(f32[1,8,128]{2,1,0:T(8,128)} %param.9) | copy-start | bytes 12292
  22.5 3.9 %collective-permute-start.1 = (f32[33,1024]{1,0:T(8,128)S(1)}, f32[33,1024]{1,0:T(8,128)S(1)}, u32[]{:S(2)}, u32[]{:S(2)}) collective-permute-start(f32[33,1024]{1,0:T(8,128)S(1)} %pad_maximum_fusion.own_ref), channel_id=1, source_target_pairs={{0,1},{1,0},{2,3},{3,2},{4,5},{5,4},{6,7},{7,6},{8,9},{9,8},{10,11... | collective-permute-start | bytes 405512 | tf_op jit(solution)/shard_map/ppermute | solution.py:292
  24.5 6.7 %collective-permute-start.2 = (f32[33,1024]{1,0:T(8,128)S(1)}, f32[33,1024]{1,0:T(8,128)S(1)}, u32[]{:S(2)}, u32[]{:S(2)}) collective-permute-start(f32[33,1024]{1,0:T(8,128)S(1)} %pad_maximum_fusion.own_ref), channel_id=1, source_target_pairs={{1,2},{2,1},{3,4},{4,3},{5,6},{6,5},{7,8},{8,7},{9,10},{10,9},{11,... | collective-permute-start | bytes 405512 | tf_op jit(solution)/shard_map/ppermute | solution.py:291
  32.8 29.3 %all-to-all-start.1 = ((f32[8,32,768]{2,1,0:T(8,128)}), f32[8,32,768]{2,1,0:T(8,128)S(1)}, u32[]{:S(2)}, u32[]{:S(2)}) async-start(f32[8,32,768]{2,1,0:T(8,128)} %bitcast.17), calls=%async_computation.1 | async-start | bytes 1572864 | tf_op jit(solution)/shard_map/all_to_all | solution.py:294
  40.1 20.1 %collective-permute-start.3 = (f32[512,128]{1,0:T(8,128)S(1)}, f32[512,128]{1,0:T(8,128)S(1)}, u32[]{:S(2)}, u32[]{:S(2)}) collective-permute-start(f32[512,128]{1,0:T(8,128)S(1)} %bitcast.18), channel_id=1, source_target_pairs={{0,256},{256,0},{1,257},{257,1},{2,258},{258,2},{3,259},{259,3},{4... | collective-permute-start | bytes 786440 | tf_op jit(solution)/shard_map/ppermute | solution.py:298
